TPU v7x, 256 devices: a whole 4x4x8 slice. The times are simulated.
256 devices in a mesh: wide: 64 (over z, y, core), lev: 4 (over x).
Axes of the slice: x: 4, y: 4, z: 8, core: 2. Of those that a mesh axis runs over, the one named last changes fastest.
Arguments:
- spec_in: bfloat16 [320, 2, 4, 641], P('wide', None, 'lev'), may hold values from -0.0068359375 to 0.0068359375
- legendre: bfloat16 [320, 641, 1280], P('wide'), may hold values from -4 to 4
- wind: bfloat16 [1280, 4, 2560], P(('wide', 'lev')), may hold values from -6 to 6
- lat_weight: float32 [1280], replicated, may hold values from 1 to 4
- wave_order: int32 [640], replicated, may hold values from 0 to 639, as said below
- lat_order: int32 [1280], replicated, may hold values from 0 to 1279, each once
- active: int32 [1280], replicated, may hold values from 5 to 640, as said below
Outputs:
- grid: bfloat16 [1280, 4, 2560], P(('wide', 'lev'))
- spec_out: float32 [320, 2, 4, 641], P('wide', None, 'lev')
Inputs may be any that keep to these rules, and one draw needn't show every extreme that they name: `wave_order`: A permutation in which slots 2p and 2p + 1 hold wavenumbers m and 639 - m. `lat_order`: each latitude once. `active`: equals 640 at some latitudes of every draw.
All inputs are finite; a program needn't handle non-finite values.
Results may differ from a plain program's by a relative error of at most 0.0072.
Values may be sent and summed in bfloat16 or wider, within the bound.
No kernel may reach another device: no remote copies, remote signals or barrier semaphores. Data moves between devices by JAX's collectives and lax.ppermute only.
A program may use at most 64 MiB of HBM per device.

v0:
```python
import math
import jax
import jax.numpy as jnp
from jax import lax
from jax.sharding import PartitionSpec as P


def make_basis(wave_order, live_count, points):
    cell_count = 4 * live_count
    cell_float = cell_count.astype(jnp.float32)
    outer_count = points // 128
    outer_ids = jnp.arange(outer_count, dtype=jnp.int32) * 128
    inner_ids = jnp.arange(128, dtype=jnp.int32)
    outer_phase = wave_order[:, None] * outer_ids[None, :] % cell_count
    inner_phase = wave_order[:, None] * inner_ids[None, :] % cell_count
    outer_angle = outer_phase.astype(jnp.float32) * (2.0 * math.pi) / cell_float
    inner_angle = inner_phase.astype(jnp.float32) * (2.0 * math.pi) / cell_float
    cos_outer = jnp.cos(outer_angle)[:, :, None]
    sin_outer = jnp.sin(outer_angle)[:, :, None]
    cos_inner = jnp.cos(inner_angle)[:, None, :]
    sin_inner = jnp.sin(inner_angle)[:, None, :]
    wave_total = wave_order.shape[0]
    cosine = (cos_outer * cos_inner - sin_outer * sin_inner).reshape(wave_total, points)
    sines = (-(sin_outer * cos_inner + cos_outer * sin_inner)).reshape(wave_total, points)
    columns = jnp.arange(points, dtype=jnp.int32)
    alive = (wave_order[:, None] < live_count) & (columns[None, :] < cell_count)
    cosine = jnp.where(alive, cosine, jnp.zeros_like(cosine))
    sines = jnp.where(alive, sines, jnp.zeros_like(sines))
    return jnp.concatenate([cosine, sines], 0).astype(jnp.bfloat16)


def legendre_direct(lat_rows, legendre, owned):
    lat_total, level_depth, parts, slot_count = lat_rows.shape
    unpacked = lat_rows.reshape(lat_total, level_depth, parts, slot_count // 2, 2)
    results = jnp.einsum("qlrps,pcq->psrlc", unpacked, legendre, preferred_element_type=jnp.float32)
    return jnp.where(owned[:, None, None, :], results[:, 0], results[:, 1])


def shards(spec_in, legendre, wind, lat_weight, wave_order, lat_order, active):
    wide_count = lax.axis_size("wide")
    lev_count = lax.axis_size("lev")
    wide_pos = lax.axis_index("wide")
    lev_pos = lax.axis_index("lev")
    pairs_here, coef_count, lat_total = legendre.shape
    wave_total = coef_count - 1
    lat_here, levels, points = wind.shape
    level_depth = spec_in.shape[2]
    local_waves = lax.dynamic_slice_in_dim(wave_order, wide_pos * 2 * pairs_here, 2 * pairs_here)
    owned = (
        jnp.arange(coef_count, dtype=jnp.int32)[None, :] < (wave_total - local_waves[0::2])[:, None]
    )
    keep_mask = owned[:, None, None, :]
    nothing = jnp.zeros_like(spec_in)
    stacked = jnp.stack(
        [jnp.where(keep_mask, spec_in, nothing), jnp.where(keep_mask, nothing, spec_in)], 1
    )
    fourier = jnp.einsum(
        "psrlc,pcq->psrlq", stacked, legendre, preferred_element_type=jnp.float32
    ).astype(jnp.bfloat16)
    ordered = jnp.take(fourier, lat_order, axis=4)
    outgoing = jnp.transpose(ordered, (4, 3, 2, 0, 1)).reshape(
        lat_total, level_depth, 2, 2 * pairs_here
    )
    arrived = lax.all_to_all(
        lax.all_to_all(outgoing, "wide", split_axis=0, concat_axis=3, tiled=True),
        "lev",
        split_axis=0,
        concat_axis=1,
        tiled=True,
    )
    first_slot = (wide_pos * lev_count + lev_pos) * lat_here
    latitudes = lax.dynamic_slice_in_dim(lat_order, first_slot, lat_here)
    counts = jnp.take(active, latitudes)
    weights = jnp.take(lat_weight, latitudes)
    factors = jnp.where(wave_order == 0, 1.0, 2.0).astype(jnp.bfloat16)

    def per_lat(inputs):
        coeffs, wind_rows, live_count, weight = inputs
        basis_rows = make_basis(wave_order, live_count, points)
        scaled = (coeffs * factors).reshape(levels, 2 * wave_total)
        grid_rows = jnp.dot(scaled, basis_rows, preferred_element_type=jnp.float32).astype(
            jnp.bfloat16
        )
        product = (grid_rows.astype(jnp.float32) * wind_rows.astype(jnp.float32)).astype(
            jnp.bfloat16
        )
        folded = lax.dot_general(
            product, basis_rows, (((1,), (1,)), ((), ())), preferred_element_type=jnp.float32
        )
        folded = (folded * (weight / (4 * live_count).astype(jnp.float32))).astype(jnp.bfloat16)
        return (grid_rows, folded.reshape(levels, 2, wave_total))

    grid, folded = lax.map(per_lat, (arrived, wind, counts, weights))
    row_ids = jnp.arange(lat_total, dtype=jnp.int32)
    received = lax.all_to_all(
        lax.all_to_all(folded, "wide", split_axis=3, concat_axis=0, tiled=True),
        "lev",
        split_axis=1,
        concat_axis=0,
        tiled=True,
    )
    lev_src = row_ids // (wide_count * lat_here)
    wide_src = row_ids // lat_here % wide_count
    within = row_ids % lat_here
    slot_index = (wide_src * lev_count + lev_src) * lat_here + within
    position = jnp.zeros((lat_total,), jnp.int32).at[jnp.take(lat_order, slot_index)].set(row_ids)
    spec_out = legendre_direct(jnp.take(received, position, axis=0), legendre, owned)
    return (grid, spec_out)


def solution(mesh):
    in_specs = (
        P("wide", None, "lev", None),
        P("wide", None, None),
        P(("wide", "lev"), None, None),
        P(),
        P(),
        P(),
        P(),
    )
    out_specs = (P(("wide", "lev"), None, None), P("wide", None, "lev", None))
    return jax.shard_map(shards, mesh=mesh, in_specs=in_specs, out_specs=out_specs, check_vma=False)
```

profile of v0, /device:TPU:1, one launch (start us, length us, event | category | flops | bytes accessed | tf_op | source)
XLA Modules:
  0.0 220.1 jit_solution(6892341236998387838)
XLA Ops:
  3.8 4.6 %fusion.38 = bf16[5,2,2,1280]{3,2,1,0:T(2,128)(2,1)S(1)} fusion(bf16[5,641,1280]{2,1,0:T(8,128)(2,1)} %param.10, bf16[5,1,2,1,641]{4,2,1,0,3:T(2,128)(2,1)S(1)} %get-tuple-element.127, bf16[5,1,2,1,641]{4,2,1,0,3:T(2,128)(2,1)S(1)} %get-tuple-element.126), kind=kOutput, calls=%fused_computation.60 | convolution fusion | flops 32896080 | bytes 8281640 | tf_op jit(solution)/shard_map/psrlc,pcq->psrlq/dot_general | solution.py:57
  9.5 4.9 %gather_fusion = bf16[1280,5,2,2]{1,3,2,0:T(2,128)(2,1)S(1)} fusion(bf16[5,2,2,1280]{0,2,3,1:T(2,128)(2,1)S(1)} %copy.62, s32[2048]{0:T(1024)S(1)} %pad_clamp_fusion.2), kind=kCustom, calls=%fused_computation | custom fusion | bytes 107520 | tf_op jit(solution)/shard_map/jit(_take)/gather | solution.py:60
  14.4 4.7 %fusion.41 = bf16[1280,1,2,5,2]{3,2,4,0,1:T(2,128)(2,1)S(1)} fusion(bf16[1280,5,2,2]{1,3,2,0:T(2,128)(2,1)S(1)} %gather_fusion, pred[1280]{0:T(1024)(128)(4,1)S(1)} %compare_and_fusion.1), kind=kLoop, calls=%fused_computation.61 | loop fusion | flops 25600 | bytes 103680 | tf_op jit(solution)/shard_map/transpose | solution.py:61
  22.5 13.2 %all-to-all-start = ((bf16[64,2,200]{2,1,0:T(2,128)(2,1)}), bf16[64,2,200]{2,1,0:T(2,128)(2,1)S(1)}, u32[]{:S(2)}, u32[]{:S(2)}) async-start(bf16[64,2,200]{2,1,0:T(2,128)(2,1)} %reshape.446), calls=%async_computation | async-start | bytes 131072 | tf_op jit(solution)/shard_map/all_to_all | solution.py:65
  35.9 7.1 %gather_fusion.3 = s32[1280]{0:T(1024)S(1)} fusion(s32[1280]{0:T(1024)S(1)} %copy-done.1, s32[2048]{0:T(1024)S(1)} %pad_clamp_fusion.1), kind=kCustom, calls=%fused_computation.3 | custom fusion | bytes 15360 | tf_op jit(solution)/shard_map/jit(_take)/gather | solution.py:106
  43.1 5.2 %scatter_custom_fusion = s32[1280]{0:T(1024)S(1)} fusion(s32[1280]{0:T(1024)S(1)} %fusion.53, s32[1280]{0:T(1024)S(1)} %iota.38, s32[]{:T(128)} %constant.119.clone.1), kind=kCustom, calls=%fused_computation.105 | custom fusion | bytes 5124 | tf_op jit(solution)/shard_map/scatter | solution.py:106
  52.6 4.0 %all-to-all-start.1 = ((bf16[20,1,2,640]{3,2,1,0:T(2,128)(2,1)}), bf16[20,1,2,640]{3,2,1,0:T(2,128)(2,1)S(1)}, u32[]{:S(2)}, u32[]{:S(2)}) async-start(bf16[20,1,2,640]{3,2,1,0:T(2,128)(2,1)} %copy.67), calls=%async_computation.1 | async-start | bytes 102400 | tf_op jit(solution)/shard_map/all_to_all | solution.py:64
  56.7 4.3 %all-to-all-done.1 = bf16[20,1,2,640]{3,2,1,0:T(2,128)(2,1)S(1)} async-done(((bf16[20,1,2,640]{3,2,1,0:T(2,128)(2,1)}), bf16[20,1,2,640]{3,2,1,0:T(2,128)(2,1)S(1)}, u32[]{:S(2)}, u32[]{:S(2)}) %all-to-all-start.1) | async-done | bytes 51232 | tf_op jit(solution)/shard_map/all_to_all | solution.py:64
  61.0 105.5 %while.12 = (s32[]{:T(128)}, bf16[5,4,2560]{2,1,0:T(4,128)(2,1)S(1)}, bf16[5,4,2,640]{3,2,1,0:T(2,128)(2,1)S(1)}, bf16[5,4,2,640]{3,2,0,1:T(2,128)(2,1)S(1)}, bf...) while((s32[]{:T(128)}, ...), condition=%wide.region_1.2_spmd, body=%wide.region_0.1_spmd.sunk | while | flops 99431064 | bytes 34495892 | solution.py:93
  62.2 4.4 %fusion.67 = (f32[640,128]{0,1:T(8,128)S(1)}, f32[640,128]{0,1:T(8,128)S(1)}) fusion(f32[]{:T(128)S(6)} %convert_element_type.93, pred[]{:T(512)S(6)} %lt.253, s32[]{:T(128)S(6)} %select_n.357, s32[640]{0:T(1024)S(1)} %get-tuple-element.233), kind=kLoop, calls=%fused_computation.28.clone.1 | loop fusion | flops 901120 | bytes 657929 | tf_op jit(solution)/shard_map/while/body/eval_jaxpr/cos | solution.py:20
  70.7 3.3 %fusion.69 = (bf16[640,2560]{0,1:T(8,128)(2,1)S(1)}, bf16[640,2560]{0,1:T(8,128)(2,1)}) fusion(bf16[640,20,128]{0,2,1:T(8,128)(2,1)S(1)} %get-tuple-element.197, pred[640]{0:T(1024)(128)(4,1)S(1)} %broadcast_compare_fusion.2, pred[2560]{0:T(1024)(128)(4,1)S(1)} %iota_compare_fusion.3, bf16[640,20,128]{0,2,1:T(8,128)(2,1)S(1)} %get-tuple-element.198), kind=kLoop, calls=%fused_computation.8.clone.1 | loop fusion | flops 4915200 | bytes 13110400 | tf_op jit(solution)/shard_map/convert.1
  74.0 3.9 %bitcast_dynamic-update-slice_fusion.2 = (bf16[5,4,2560]{2,1,0:T(4,128)(2,1)S(1)}, bf16[4,2560]{1,0:T(4,128)(2,1)}) fusion(bf16[5,4,2560]{2,1,0:T(4,128)(2,1)S(1)} %get-tuple-element.216, s32[]{:T(128)} %get-tuple-element.215, bf16[640,2560]{0,1:T(8,128)(2,1)} %get-tuple-element.199, bf16[640,2560]{0,1:T(8,128)(2,1)S(1)} %get-tuple-element.200, ...), kind=kOutput, calls=%fused_computation.43.clone.1 | convolution fusion | flops 39352320 | bytes 6608900 | tf_op jit(solution)/shard_map/while/body/eval_jaxpr/dot_general | solution.py:81
  79.1 2.9 %fusion.70 = bf16[4,1280]{1,0:T(4,128)(2,1)S(1)} fusion(bf16[640,2560]{0,1:T(8,128)(2,1)} %get-tuple-element.199, bf16[640,2560]{0,1:T(8,128)(2,1)S(1)} %get-tuple-element.200, bf16[4,2560]{1,0:T(4,128)(2,1)} %get-tuple-element.202, bf16[5,4,2560]{2,1,0:T(4,128)(2,1)} %get-tuple-element.234, s32[]{:T(128)} %get-tuple-element.215, f32[]{:T(128)S(6)} %div.124), kind=kOutput, calls=%fused_computation.17.clone.1 | convolution fusion | flops 39372800 | bytes 6605316 | tf_op jit(solution)/shard_map/while/body/eval_jaxpr/dot_general | solution.py:87
  83.3 4.4 %fusion.67 = (f32[640,128]{0,1:T(8,128)S(1)}, f32[640,128]{0,1:T(8,128)S(1)}) fusion(f32[]{:T(128)S(6)} %convert_element_type.93, pred[]{:T(512)S(6)} %lt.253, s32[]{:T(128)S(6)} %select_n.357, s32[640]{0:T(1024)S(1)} %get-tuple-element.233), kind=kLoop, calls=%fused_computation.28.clone.1 | loop fusion | flops 901120 | bytes 657929 | tf_op jit(solution)/shard_map/while/body/eval_jaxpr/cos | solution.py:20
  91.8 3.3 %fusion.69 = (bf16[640,2560]{0,1:T(8,128)(2,1)S(1)}, bf16[640,2560]{0,1:T(8,128)(2,1)}) fusion(bf16[640,20,128]{0,2,1:T(8,128)(2,1)S(1)} %get-tuple-element.197, pred[640]{0:T(1024)(128)(4,1)S(1)} %broadcast_compare_fusion.2, pred[2560]{0:T(1024)(128)(4,1)S(1)} %iota_compare_fusion.3, bf16[640,20,128]{0,2,1:T(8,128)(2,1)S(1)} %get-tuple-element.198), kind=kLoop, calls=%fused_computation.8.clone.1 | loop fusion | flops 4915200 | bytes 13110400 | tf_op jit(solution)/shard_map/convert.1
  95.1 3.9 %bitcast_dynamic-update-slice_fusion.2 = (bf16[5,4,2560]{2,1,0:T(4,128)(2,1)S(1)}, bf16[4,2560]{1,0:T(4,128)(2,1)}) fusion(bf16[5,4,2560]{2,1,0:T(4,128)(2,1)S(1)} %get-tuple-element.216, s32[]{:T(128)} %get-tuple-element.215, bf16[640,2560]{0,1:T(8,128)(2,1)} %get-tuple-element.199, bf16[640,2560]{0,1:T(8,128)(2,1)S(1)} %get-tuple-element.200, ...), kind=kOutput, calls=%fused_computation.43.clone.1 | convolution fusion | flops 39352320 | bytes 6608900 | tf_op jit(solution)/shard_map/while/body/eval_jaxpr/dot_general | solution.py:81
  104.4 4.4 %fusion.67 = (f32[640,128]{0,1:T(8,128)S(1)}, f32[640,128]{0,1:T(8,128)S(1)}) fusion(f32[]{:T(128)S(6)} %convert_element_type.93, pred[]{:T(512)S(6)} %lt.253, s32[]{:T(128)S(6)} %select_n.357, s32[640]{0:T(1024)S(1)} %get-tuple-element.233), kind=kLoop, calls=%fused_computation.28.clone.1 | loop fusion | flops 901120 | bytes 657929 | tf_op jit(solution)/shard_map/while/body/eval_jaxpr/cos | solution.py:20
  112.9 3.3 %fusion.69 = (bf16[640,2560]{0,1:T(8,128)(2,1)S(1)}, bf16[640,2560]{0,1:T(8,128)(2,1)}) fusion(bf16[640,20,128]{0,2,1:T(8,128)(2,1)S(1)} %get-tuple-element.197, pred[640]{0:T(1024)(128)(4,1)S(1)} %broadcast_compare_fusion.2, pred[2560]{0:T(1024)(128)(4,1)S(1)} %iota_compare_fusion.3, bf16[640,20,128]{0,2,1:T(8,128)(2,1)S(1)} %get-tuple-element.198), kind=kLoop, calls=%fused_computation.8.clone.1 | loop fusion | flops 4915200 | bytes 13110400 | tf_op jit(solution)/shard_map/convert.1
  116.2 3.9 %bitcast_dynamic-update-slice_fusion.2 = (bf16[5,4,2560]{2,1,0:T(4,128)(2,1)S(1)}, bf16[4,2560]{1,0:T(4,128)(2,1)}) fusion(bf16[5,4,2560]{2,1,0:T(4,128)(2,1)S(1)} %get-tuple-element.216, s32[]{:T(128)} %get-tuple-element.215, bf16[640,2560]{0,1:T(8,128)(2,1)} %get-tuple-element.199, bf16[640,2560]{0,1:T(8,128)(2,1)S(1)} %get-tuple-element.200, ...), kind=kOutput, calls=%fused_computation.43.clone.1 | convolution fusion | flops 39352320 | bytes 6608900 | tf_op jit(solution)/shard_map/while/body/eval_jaxpr/dot_general | solution.py:81
  125.5 4.4 %fusion.67 = (f32[640,128]{0,1:T(8,128)S(1)}, f32[640,128]{0,1:T(8,128)S(1)}) fusion(f32[]{:T(128)S(6)} %convert_element_type.93, pred[]{:T(512)S(6)} %lt.253, s32[]{:T(128)S(6)} %select_n.357, s32[640]{0:T(1024)S(1)} %get-tuple-element.233), kind=kLoop, calls=%fused_computation.28.clone.1 | loop fusion | flops 901120 | bytes 657929 | tf_op jit(solution)/shard_map/while/body/eval_jaxpr/cos | solution.py:20
  134.0 3.3 %fusion.69 = (bf16[640,2560]{0,1:T(8,128)(2,1)S(1)}, bf16[640,2560]{0,1:T(8,128)(2,1)}) fusion(bf16[640,20,128]{0,2,1:T(8,128)(2,1)S(1)} %get-tuple-element.197, pred[640]{0:T(1024)(128)(4,1)S(1)} %broadcast_compare_fusion.2, pred[2560]{0:T(1024)(128)(4,1)S(1)} %iota_compare_fusion.3, bf16[640,20,128]{0,2,1:T(8,128)(2,1)S(1)} %get-tuple-element.198), kind=kLoop, calls=%fused_computation.8.clone.1 | loop fusion | flops 4915200 | bytes 13110400 | tf_op jit(solution)/shard_map/convert.1
  137.3 3.9 %bitcast_dynamic-update-slice_fusion.2 = (bf16[5,4,2560]{2,1,0:T(4,128)(2,1)S(1)}, bf16[4,2560]{1,0:T(4,128)(2,1)}) fusion(bf16[5,4,2560]{2,1,0:T(4,128)(2,1)S(1)} %get-tuple-element.216, s32[]{:T(128)} %get-tuple-element.215, bf16[640,2560]{0,1:T(8,128)(2,1)} %get-tuple-element.199, bf16[640,2560]{0,1:T(8,128)(2,1)S(1)} %get-tuple-element.200, ...), kind=kOutput, calls=%fused_computation.43.clone.1 | convolution fusion | flops 39352320 | bytes 6608900 | tf_op jit(solution)/shard_map/while/body/eval_jaxpr/dot_general | solution.py:81
  146.6 4.4 %fusion.67 = (f32[640,128]{0,1:T(8,128)S(1)}, f32[640,128]{0,1:T(8,128)S(1)}) fusion(f32[]{:T(128)S(6)} %convert_element_type.93, pred[]{:T(512)S(6)} %lt.253, s32[]{:T(128)S(6)} %select_n.357, s32[640]{0:T(1024)S(1)} %get-tuple-element.233), kind=kLoop, calls=%fused_computation.28.clone.1 | loop fusion | flops 901120 | bytes 657929 | tf_op jit(solution)/shard_map/while/body/eval_jaxpr/cos | solution.py:20
  155.1 3.3 %fusion.69 = (bf16[640,2560]{0,1:T(8,128)(2,1)S(1)}, bf16[640,2560]{0,1:T(8,128)(2,1)}) fusion(bf16[640,20,128]{0,2,1:T(8,128)(2,1)S(1)} %get-tuple-element.197, pred[640]{0:T(1024)(128)(4,1)S(1)} %broadcast_compare_fusion.2, pred[2560]{0:T(1024)(128)(4,1)S(1)} %iota_compare_fusion.3, bf16[640,20,128]{0,2,1:T(8,128)(2,1)S(1)} %get-tuple-element.198), kind=kLoop, calls=%fused_computation.8.clone.1 | loop fusion | flops 4915200 | bytes 13110400 | tf_op jit(solution)/shard_map/convert.1
  158.4 3.9 %bitcast_dynamic-update-slice_fusion.2 = (bf16[5,4,2560]{2,1,0:T(4,128)(2,1)S(1)}, bf16[4,2560]{1,0:T(4,128)(2,1)}) fusion(bf16[5,4,2560]{2,1,0:T(4,128)(2,1)S(1)} %get-tuple-element.216, s32[]{:T(128)} %get-tuple-element.215, bf16[640,2560]{0,1:T(8,128)(2,1)} %get-tuple-element.199, bf16[640,2560]{0,1:T(8,128)(2,1)S(1)} %get-tuple-element.200, ...), kind=kOutput, calls=%fused_computation.43.clone.1 | convolution fusion | flops 39352320 | bytes 6608900 | tf_op jit(solution)/shard_map/while/body/eval_jaxpr/dot_general | solution.py:81
  170.3 11.7 %all-to-all-start.2 = ((bf16[64,2,200]{2,1,0:T(2,128)(2,1)}), bf16[64,2,200]{2,1,0:T(2,128)(2,1)S(1)}, u32[]{:S(2)}, u32[]{:S(2)}) async-start(bf16[64,2,200]{2,1,0:T(2,128)(2,1)} %reshape.448), calls=%async_computation.2 | async-start | bytes 131072 | tf_op jit(solution)/shard_map/all_to_all | solution.py:96
  182.0 10.1 %all-to-all-done.2 = bf16[64,2,200]{2,1,0:T(2,128)(2,1)S(1)} async-done(((bf16[64,2,200]{2,1,0:T(2,128)(2,1)}), bf16[64,2,200]{2,1,0:T(2,128)(2,1)S(1)}, u32[]{:S(2)}, u32[]{:S(2)}) %all-to-all-start.2) | async-done | bytes 51232 | tf_op jit(solution)/shard_map/all_to_all | solution.py:96
  193.0 5.7 %copy.80 = bf16[5,4,2,64,10]{4,3,2,1,0:T(8,128)(2,1)S(1)} copy(bf16[5,4,2,64,10]{0,1,2,4,3:T(4,128)(2,1)S(1)} %bitcast.99) | data formatting | bytes 102400 | tf_op jit(solution)/shard_map/all_to_all | solution.py:96
  200.6 3.3 %all-to-all-start.3 = ((bf16[320,4,2,10]{0,2,3,1:T(2,128)(2,1)}), bf16[320,4,2,10]{0,2,3,1:T(2,128)(2,1)S(1)}, u32[]{:S(2)}, u32[]{:S(2)}) async-start(bf16[320,4,2,10]{0,2,3,1:T(2,128)(2,1)} %copy.72), calls=%async_computation.3 | async-start | bytes 122880 | tf_op jit(solution)/shard_map/all_to_all | solution.py:95
  203.9 4.4 %all-to-all-done.3 = bf16[320,4,2,10]{0,2,3,1:T(2,128)(2,1)S(1)} async-done(((bf16[320,4,2,10]{0,2,3,1:T(2,128)(2,1)}), bf16[320,4,2,10]{0,2,3,1:T(2,128)(2,1)S(1)}, u32[]{:S(2)}, u32[]{:S(2)}) %all-to-all-start.3) | async-done | bytes 51232 | tf_op jit(solution)/shard_map/all_to_all | solution.py:95
  208.9 4.4 %gather_fusion.4 = bf16[1280,2,10]{2,1,0:T(2,128)(2,1)S(1)} fusion(bf16[1280,2,10]{2,1,0:T(2,128)(2,1)S(1)} %bitcast.100, s32[2048]{0:T(1024)S(1)} %pad_clamp_fusion), kind=kCustom, calls=%fused_computation.4 | custom fusion | bytes 107520 | tf_op jit(solution)/shard_map/jit(_take)/gather | solution.py:107
  213.8 5.6 %fusion.42 = f32[5,2,2,1,641]{4,2,0,3,1:T(2,128)S(1)} fusion(bf16[5,641,1280]{2,1,0:T(8,128)(2,1)} %param.10, bf16[1280,2,5,2]{0,1,3,2:T(2,128)(2,1)S(1)} %bitcast.107, pred[1280]{0:T(1024)(128)(4,1)S(1)} %compare_and_fusion), kind=kOutput, calls=%fused_computation.62 | convolution fusion | flops 32844800 | bytes 8308560 | tf_op jit(solution)/shard_map/qlrps,pcq->psrlc/dot_general | solution.py:35
  (121 shorter events, 58.5 us)
Async XLA Ops:
  0.6 47.7 %copy-start = (f32[1280]{0:T(1024)S(1)}, f32[1280]{0:T(1024)}, u32[]{:S(2)}) copy-start(f32[1280]{0:T(1024)} %param.12) | copy-start | bytes 15364
  3.8 31.9 %copy-start.3 = (s32[640]{0:T(1024)S(1)}, s32[640]{0:T(1024)}, u32[]{:S(2)}) copy-start(s32[640]{0:T(1024)} %param.13) | copy-start | bytes 7684
  3.8 32.0 %copy-start.1 = (s32[1280]{0:T(1024)S(1)}, s32[1280]{0:T(1024)}, u32[]{:S(2)}) copy-start(s32[1280]{0:T(1024)} %param.14) | copy-start | bytes 15364
  19.1 30.0 %copy-start.2 = (s32[1280]{0:T(1024)S(1)}, s32[1280]{0:T(1024)}, u32[]{:S(2)}) copy-start(s32[1280]{0:T(1024)} %param.15) | copy-start | bytes 15364
  22.5 27.2 %all-to-all-start = ((bf16[64,2,200]{2,1,0:T(2,128)(2,1)}), bf16[64,2,200]{2,1,0:T(2,128)(2,1)S(1)}, u32[]{:S(2)}, u32[]{:S(2)}) async-start(bf16[64,2,200]{2,1,0:T(2,128)(2,1)} %reshape.446), calls=%async_computation | async-start | bytes 131072 | tf_op jit(solution)/shard_map/all_to_all | solution.py:65
  52.6 8.4 %all-to-all-start.1 = ((bf16[20,1,2,640]{3,2,1,0:T(2,128)(2,1)}), bf16[20,1,2,640]{3,2,1,0:T(2,128)(2,1)S(1)}, u32[]{:S(2)}, u32[]{:S(2)}) async-start(bf16[20,1,2,640]{3,2,1,0:T(2,128)(2,1)} %copy.67), calls=%async_computation.1 | async-start | bytes 102400 | tf_op jit(solution)/shard_map/all_to_all | solution.py:64
  166.5 52.9 %copy-start.4 = (bf16[5,4,2560]{2,1,0:T(4,128)(2,1)}, bf16[5,4,2560]{2,1,0:T(4,128)(2,1)S(1)}, u32[]{:S(2)}) copy-start(bf16[5,4,2560]{2,1,0:T(4,128)(2,1)S(1)} %get-tuple-element.96) | copy-start | bytes 307204
  170.3 21.8 %all-to-all-start.2 = ((bf16[64,2,200]{2,1,0:T(2,128)(2,1)}), bf16[64,2,200]{2,1,0:T(2,128)(2,1)S(1)}, u32[]{:S(2)}, u32[]{:S(2)}) async-start(bf16[64,2,200]{2,1,0:T(2,128)(2,1)} %reshape.448), calls=%async_computation.2 | async-start | bytes 131072 | tf_op jit(solution)/shard_map/all_to_all | solution.py:96
  200.6 7.7 %all-to-all-start.3 = ((bf16[320,4,2,10]{0,2,3,1:T(2,128)(2,1)}), bf16[320,4,2,10]{0,2,3,1:T(2,128)(2,1)S(1)}, u32[]{:S(2)}, u32[]{:S(2)}) async-start(bf16[320,4,2,10]{0,2,3,1:T(2,128)(2,1)} %copy.72), calls=%async_computation.3 | async-start | bytes 122880 | tf_op jit(solution)/shard_map/all_to_all | solution.py:95
where the time goes:
time: 221 us; the launch traced here: 220 us
  other arithmetic  65.8 us (30%)
  local copies, waits for them, and re-layouts  51.2 us (23%)
  matrix products  44.2 us (20%)
  starting transfers between devices  32.2 us (15%)
  waiting for transfers between devices  18.8 us (9%)
  loops' own time  6.96 us (3%)
    cos x5, other arithmetic, make_basis(): cos_inner = jnp.cos(inner_angle)[:, None, :]  21.8 us
    dot_general x5, matrix products, per_lat(): jnp.dot(scaled, basis_rows, preferred_element_type=jnp.float32)  19.4 us
    another operation x5, other arithmetic  16.4 us
    dot_general x5, matrix products, per_lat(): lax.dot_general(product, basis_rows, (((1,), (1,)), ((), ())), preferred_...  14.6 us
    all_to_all x1, starting transfers between devices, shards(): lax.all_to_all(outgoing, 'wide', split_axis=0, concat_axis=3, tiled=True)  13.2 us
    sub x5, other arithmetic, make_basis(): cos_outer * cos_inner - sin_outer * sin_inner  12.1 us
    all_to_all x1, starting transfers between devices, shards(): lax.all_to_all(folded, 'wide', split_axis=3, concat_axis=0, tiled=True)  11.7 us
    all_to_all x1, waiting for transfers between devices, shards(): lax.all_to_all(folded, 'wide', split_axis=3, concat_axis=0, tiled=True)  10.1 us
  transfers between devices with their start and end apart: 4, of which 3 were waited for; matrix products, arithmetic and copies ran while one was open for 6% of the time, Pallas kernels for 0%

commit v1 on v0

--- a/solution.py
+++ b/solution.py
@@ -61,13 +61,10 @@
     outgoing = jnp.transpose(ordered, (4, 3, 2, 0, 1)).reshape(
         lat_total, level_depth, 2, 2 * pairs_here
     )
-    arrived = lax.all_to_all(
-        lax.all_to_all(outgoing, "wide", split_axis=0, concat_axis=3, tiled=True),
-        "lev",
-        split_axis=0,
-        concat_axis=1,
-        tiled=True,
-    )
+    block = lax.all_to_all(outgoing, "wide", split_axis=0, concat_axis=3, tiled=True)
+    pieces = jnp.split(block, lax.axis_size("lev"), axis=0)
+    incoming = lax.all_to_all(jnp.stack(pieces), "lev", 0, 0)
+    arrived = jnp.concatenate(incoming, axis=1)
     first_slot = (wide_pos * lev_count + lev_pos) * lat_here
     latitudes = lax.dynamic_slice_in_dim(lat_order, first_slot, lat_here)
     counts = jnp.take(active, latitudes)

time: 221 us -> 227 us (1.027)
  local copies, waits for them, and re-layouts: 51.2 us -> 55.9 us
    split x0 -> x5, local copies, waits for them, and re-layouts: none -> 4.61 us  [shards(): pieces = jnp.split(block, lax.axis_size('lev'), axis=0)]
    another operation x5 -> x6, other arithmetic: 16.4 us -> 17.1 us
where the time goes in v1:
time: 227 us; the launch traced here: 226 us
  other arithmetic  66.6 us (29%)
  local copies, waits for them, and re-layouts  55.9 us (25%)
  matrix products  44.2 us (19%)
  starting transfers between devices  32.2 us (14%)
  waiting for transfers between devices  18.8 us (8%)
  loops' own time  6.96 us (3%)
    cos x5, other arithmetic, make_basis(): cos_inner = jnp.cos(inner_angle)[:, None, :]  21.8 us
    dot_general x5, matrix products, per_lat(): jnp.dot(scaled, basis_rows, preferred_element_type=jnp.float32)  19.4 us
    another operation x5, other arithmetic  16.4 us
    dot_general x5, matrix products, per_lat(): lax.dot_general(product, basis_rows, (((1,), (1,)), ((), ())), preferred_...  14.6 us
    all_to_all x1, starting transfers between devices, shards(): lax.all_to_all(outgoing, 'wide', split_axis=0, concat_axis=3, tiled=True)  13.2 us
    sub x5, other arithmetic, make_basis(): cos_outer * cos_inner - sin_outer * sin_inner  12.2 us
    all_to_all x1, starting transfers between devices, shards(): lax.all_to_all(folded, 'wide', split_axis=3, concat_axis=0, tiled=True)  11.7 us
    all_to_all x1, waiting for transfers between devices, shards(): lax.all_to_all(folded, 'wide', split_axis=3, concat_axis=0, tiled=True)  10.1 us
  transfers between devices with their start and end apart: 4, of which 3 were waited for; matrix products, arithmetic and copies ran while one was open for 6% of the time, Pallas kernels for 0%

profile of v1, /device:TPU:1, one launch (start us, length us, event | category | flops | bytes accessed | tf_op | source)
XLA Modules:
  0.0 225.7 jit_solution(4414157471503090915)
XLA Ops:
  3.8 4.6 %fusion.38 = bf16[5,2,2,1280]{3,2,1,0:T(2,128)(2,1)S(1)} fusion(bf16[5,641,1280]{2,1,0:T(8,128)(2,1)} %param.10, bf16[5,1,2,1,641]{4,2,1,0,3:T(2,128)(2,1)S(1)} %get-tuple-element.131, bf16[5,1,2,1,641]{4,2,1,0,3:T(2,128)(2,1)S(1)} %get-tuple-element.130), kind=kOutput, calls=%fused_computation.60 | convolution fusion | flops 32896080 | bytes 8281640 | tf_op jit(solution)/shard_map/psrlc,pcq->psrlq/dot_general | solution.py:57
  9.5 4.9 %gather_fusion = bf16[1280,5,2,2]{1,3,2,0:T(2,128)(2,1)S(1)} fusion(bf16[5,2,2,1280]{0,2,3,1:T(2,128)(2,1)S(1)} %copy.69, s32[2048]{0:T(1024)S(1)} %pad_clamp_fusion.2), kind=kCustom, calls=%fused_computation | custom fusion | bytes 107520 | tf_op jit(solution)/shard_map/jit(_take)/gather | solution.py:60
  14.4 4.7 %fusion.41 = bf16[1280,1,2,5,2]{3,2,4,0,1:T(2,128)(2,1)S(1)} fusion(bf16[1280,5,2,2]{1,3,2,0:T(2,128)(2,1)S(1)} %gather_fusion, pred[1280]{0:T(1024)(128)(4,1)S(1)} %compare_and_fusion.1), kind=kLoop, calls=%fused_computation.61 | loop fusion | flops 25600 | bytes 103680 | tf_op jit(solution)/shard_map/transpose | solution.py:61
  22.5 13.2 %all-to-all-start = ((bf16[64,2,200]{2,1,0:T(2,128)(2,1)}), bf16[64,2,200]{2,1,0:T(2,128)(2,1)S(1)}, u32[]{:S(2)}, u32[]{:S(2)}) async-start(bf16[64,2,200]{2,1,0:T(2,128)(2,1)} %reshape.462), calls=%async_computation | async-start | bytes 131072 | tf_op jit(solution)/shard_map/all_to_all | solution.py:64
  35.9 7.1 %gather_fusion.3 = s32[1280]{0:T(1024)S(1)} fusion(s32[1280]{0:T(1024)S(1)} %copy-done.1, s32[2048]{0:T(1024)S(1)} %pad_clamp_fusion.1), kind=kCustom, calls=%fused_computation.3 | custom fusion | bytes 15360 | tf_op jit(solution)/shard_map/jit(_take)/gather | solution.py:103
  43.0 5.4 %scatter_custom_fusion = s32[1280]{0:T(1024)S(1)} fusion(s32[1280]{0:T(1024)S(1)} %fusion.53, s32[1280]{0:T(1024)S(1)} %iota.38, s32[]{:T(128)} %constant.119.clone.1), kind=kCustom, calls=%fused_computation.106 | custom fusion | bytes 5124 | tf_op jit(solution)/shard_map/scatter | solution.py:103
  58.0 4.0 %all-to-all-start.1 = ((bf16[4,5,1,2,640]{4,3,1,2,0:T(2,128)(2,1)}), bf16[4,5,1,2,640]{4,3,1,2,0:T(2,128)(2,1)S(1)}, u32[]{:S(2)}, u32[]{:S(2)}) async-start(bf16[4,5,1,2,640]{4,3,1,2,0:T(2,128)(2,1)} %pad_maximum_fusion.9), calls=%async_computation.1 | async-start | bytes 102400 | tf_op jit(solution)/shard_map/all_to_all | solution.py:66
  62.1 4.3 %all-to-all-done.1 = bf16[4,5,1,2,640]{4,3,1,2,0:T(2,128)(2,1)S(1)} async-done(((bf16[4,5,1,2,640]{4,3,1,2,0:T(2,128)(2,1)}), bf16[4,5,1,2,640]{4,3,1,2,0:T(2,128)(2,1)S(1)}, u32[]{:S(2)}, u32[]{:S(2)}) %all-to-all-start.1) | async-done | bytes 51232 | tf_op jit(solution)/shard_map/all_to_all | solution.py:66
  66.4 105.5 %while.12 = (s32[]{:T(128)}, bf16[5,4,2560]{2,1,0:T(4,128)(2,1)S(1)}, bf16[5,4,2,640]{3,2,1,0:T(2,128)(2,1)S(1)}, bf16[5,4,2,640]{3,2,0,1:T(2,128)(2,1)S(1)}, bf...) while((s32[]{:T(128)}, ...), condition=%wide.region_1.2_spmd, body=%wide.region_0.1_spmd.sunk | while | flops 99431064 | bytes 34495892 | solution.py:90
  67.7 4.4 %fusion.68 = (f32[640,128]{0,1:T(8,128)S(1)}, f32[640,128]{0,1:T(8,128)S(1)}) fusion(f32[]{:T(128)S(6)} %convert_element_type.93, pred[]{:T(512)S(6)} %lt.253, s32[]{:T(128)S(6)} %select_n.357, s32[640]{0:T(1024)S(1)} %get-tuple-element.237), kind=kLoop, calls=%fused_computation.28.clone.1 | loop fusion | flops 901120 | bytes 657929 | tf_op jit(solution)/shard_map/while/body/eval_jaxpr/cos | solution.py:20
  76.1 3.3 %fusion.70 = (bf16[640,2560]{0,1:T(8,128)(2,1)S(1)}, bf16[640,2560]{0,1:T(8,128)(2,1)}) fusion(bf16[640,20,128]{0,2,1:T(8,128)(2,1)S(1)} %get-tuple-element.201, pred[640]{0:T(1024)(128)(4,1)S(1)} %broadcast_compare_fusion.2, pred[2560]{0:T(1024)(128)(4,1)S(1)} %iota_compare_fusion.3, bf16[640,20,128]{0,2,1:T(8,128)(2,1)S(1)} %get-tuple-element.202), kind=kLoop, calls=%fused_computation.8.clone.1 | loop fusion | flops 4915200 | bytes 13110400 | tf_op jit(solution)/shard_map/convert.1
  79.5 3.9 %bitcast_dynamic-update-slice_fusion.2 = (bf16[5,4,2560]{2,1,0:T(4,128)(2,1)S(1)}, bf16[4,2560]{1,0:T(4,128)(2,1)}) fusion(bf16[5,4,2560]{2,1,0:T(4,128)(2,1)S(1)} %get-tuple-element.220, s32[]{:T(128)} %get-tuple-element.219, bf16[640,2560]{0,1:T(8,128)(2,1)} %get-tuple-element.203, bf16[640,2560]{0,1:T(8,128)(2,1)S(1)} %get-tuple-element.204, ...), kind=kOutput, calls=%fused_computation.43.clone.1 | convolution fusion | flops 39352320 | bytes 6608900 | tf_op jit(solution)/shard_map/while/body/eval_jaxpr/dot_general | solution.py:78
  84.6 2.9 %fusion.71 = bf16[4,1280]{1,0:T(4,128)(2,1)S(1)} fusion(bf16[640,2560]{0,1:T(8,128)(2,1)} %get-tuple-element.203, bf16[640,2560]{0,1:T(8,128)(2,1)S(1)} %get-tuple-element.204, bf16[4,2560]{1,0:T(4,128)(2,1)} %get-tuple-element.206, bf16[5,4,2560]{2,1,0:T(4,128)(2,1)} %get-tuple-element.238, s32[]{:T(128)} %get-tuple-element.219, f32[]{:T(128)S(6)} %div.124), kind=kOutput, calls=%fused_computation.17.clone.1 | convolution fusion | flops 39372800 | bytes 6605316 | tf_op jit(solution)/shard_map/while/body/eval_jaxpr/dot_general | solution.py:84
  88.8 4.4 %fusion.68 = (f32[640,128]{0,1:T(8,128)S(1)}, f32[640,128]{0,1:T(8,128)S(1)}) fusion(f32[]{:T(128)S(6)} %convert_element_type.93, pred[]{:T(512)S(6)} %lt.253, s32[]{:T(128)S(6)} %select_n.357, s32[640]{0:T(1024)S(1)} %get-tuple-element.237), kind=kLoop, calls=%fused_computation.28.clone.1 | loop fusion | flops 901120 | bytes 657929 | tf_op jit(solution)/shard_map/while/body/eval_jaxpr/cos | solution.py:20
  97.2 3.3 %fusion.70 = (bf16[640,2560]{0,1:T(8,128)(2,1)S(1)}, bf16[640,2560]{0,1:T(8,128)(2,1)}) fusion(bf16[640,20,128]{0,2,1:T(8,128)(2,1)S(1)} %get-tuple-element.201, pred[640]{0:T(1024)(128)(4,1)S(1)} %broadcast_compare_fusion.2, pred[2560]{0:T(1024)(128)(4,1)S(1)} %iota_compare_fusion.3, bf16[640,20,128]{0,2,1:T(8,128)(2,1)S(1)} %get-tuple-element.202), kind=kLoop, calls=%fused_computation.8.clone.1 | loop fusion | flops 4915200 | bytes 13110400 | tf_op jit(solution)/shard_map/convert.1
  100.6 3.9 %bitcast_dynamic-update-slice_fusion.2 = (bf16[5,4,2560]{2,1,0:T(4,128)(2,1)S(1)}, bf16[4,2560]{1,0:T(4,128)(2,1)}) fusion(bf16[5,4,2560]{2,1,0:T(4,128)(2,1)S(1)} %get-tuple-element.220, s32[]{:T(128)} %get-tuple-element.219, bf16[640,2560]{0,1:T(8,128)(2,1)} %get-tuple-element.203, bf16[640,2560]{0,1:T(8,128)(2,1)S(1)} %get-tuple-element.204, ...), kind=kOutput, calls=%fused_computation.43.clone.1 | convolution fusion | flops 39352320 | bytes 6608900 | tf_op jit(solution)/shard_map/while/body/eval_jaxpr/dot_general | solution.py:78
  109.9 4.4 %fusion.68 = (f32[640,128]{0,1:T(8,128)S(1)}, f32[640,128]{0,1:T(8,128)S(1)}) fusion(f32[]{:T(128)S(6)} %convert_element_type.93, pred[]{:T(512)S(6)} %lt.253, s32[]{:T(128)S(6)} %select_n.357, s32[640]{0:T(1024)S(1)} %get-tuple-element.237), kind=kLoop, calls=%fused_computation.28.clone.1 | loop fusion | flops 901120 | bytes 657929 | tf_op jit(solution)/shard_map/while/body/eval_jaxpr/cos | solution.py:20
  118.3 3.3 %fusion.70 = (bf16[640,2560]{0,1:T(8,128)(2,1)S(1)}, bf16[640,2560]{0,1:T(8,128)(2,1)}) fusion(bf16[640,20,128]{0,2,1:T(8,128)(2,1)S(1)} %get-tuple-element.201, pred[640]{0:T(1024)(128)(4,1)S(1)} %broadcast_compare_fusion.2, pred[2560]{0:T(1024)(128)(4,1)S(1)} %iota_compare_fusion.3, bf16[640,20,128]{0,2,1:T(8,128)(2,1)S(1)} %get-tuple-element.202), kind=kLoop, calls=%fused_computation.8.clone.1 | loop fusion | flops 4915200 | bytes 13110400 | tf_op jit(solution)/shard_map/convert.1
  121.7 3.9 %bitcast_dynamic-update-slice_fusion.2 = (bf16[5,4,2560]{2,1,0:T(4,128)(2,1)S(1)}, bf16[4,2560]{1,0:T(4,128)(2,1)}) fusion(bf16[5,4,2560]{2,1,0:T(4,128)(2,1)S(1)} %get-tuple-element.220, s32[]{:T(128)} %get-tuple-element.219, bf16[640,2560]{0,1:T(8,128)(2,1)} %get-tuple-element.203, bf16[640,2560]{0,1:T(8,128)(2,1)S(1)} %get-tuple-element.204, ...), kind=kOutput, calls=%fused_computation.43.clone.1 | convolution fusion | flops 39352320 | bytes 6608900 | tf_op jit(solution)/shard_map/while/body/eval_jaxpr/dot_general | solution.py:78
  131.0 4.4 %fusion.68 = (f32[640,128]{0,1:T(8,128)S(1)}, f32[640,128]{0,1:T(8,128)S(1)}) fusion(f32[]{:T(128)S(6)} %convert_element_type.93, pred[]{:T(512)S(6)} %lt.253, s32[]{:T(128)S(6)} %select_n.357, s32[640]{0:T(1024)S(1)} %get-tuple-element.237), kind=kLoop, calls=%fused_computation.28.clone.1 | loop fusion | flops 901120 | bytes 657929 | tf_op jit(solution)/shard_map/while/body/eval_jaxpr/cos | solution.py:20
  139.5 3.3 %fusion.70 = (bf16[640,2560]{0,1:T(8,128)(2,1)S(1)}, bf16[640,2560]{0,1:T(8,128)(2,1)}) fusion(bf16[640,20,128]{0,2,1:T(8,128)(2,1)S(1)} %get-tuple-element.201, pred[640]{0:T(1024)(128)(4,1)S(1)} %broadcast_compare_fusion.2, pred[2560]{0:T(1024)(128)(4,1)S(1)} %iota_compare_fusion.3, bf16[640,20,128]{0,2,1:T(8,128)(2,1)S(1)} %get-tuple-element.202), kind=kLoop, calls=%fused_computation.8.clone.1 | loop fusion | flops 4915200 | bytes 13110400 | tf_op jit(solution)/shard_map/convert.1
  142.8 3.9 %bitcast_dynamic-update-slice_fusion.2 = (bf16[5,4,2560]{2,1,0:T(4,128)(2,1)S(1)}, bf16[4,2560]{1,0:T(4,128)(2,1)}) fusion(bf16[5,4,2560]{2,1,0:T(4,128)(2,1)S(1)} %get-tuple-element.220, s32[]{:T(128)} %get-tuple-element.219, bf16[640,2560]{0,1:T(8,128)(2,1)} %get-tuple-element.203, bf16[640,2560]{0,1:T(8,128)(2,1)S(1)} %get-tuple-element.204, ...), kind=kOutput, calls=%fused_computation.43.clone.1 | convolution fusion | flops 39352320 | bytes 6608900 | tf_op jit(solution)/shard_map/while/body/eval_jaxpr/dot_general | solution.py:78
  152.1 4.4 %fusion.68 = (f32[640,128]{0,1:T(8,128)S(1)}, f32[640,128]{0,1:T(8,128)S(1)}) fusion(f32[]{:T(128)S(6)} %convert_element_type.93, pred[]{:T(512)S(6)} %lt.253, s32[]{:T(128)S(6)} %select_n.357, s32[640]{0:T(1024)S(1)} %get-tuple-element.237), kind=kLoop, calls=%fused_computation.28.clone.1 | loop fusion | flops 901120 | bytes 657929 | tf_op jit(solution)/shard_map/while/body/eval_jaxpr/cos | solution.py:20
  160.6 3.3 %fusion.70 = (bf16[640,2560]{0,1:T(8,128)(2,1)S(1)}, bf16[640,2560]{0,1:T(8,128)(2,1)}) fusion(bf16[640,20,128]{0,2,1:T(8,128)(2,1)S(1)} %get-tuple-element.201, pred[640]{0:T(1024)(128)(4,1)S(1)} %broadcast_compare_fusion.2, pred[2560]{0:T(1024)(128)(4,1)S(1)} %iota_compare_fusion.3, bf16[640,20,128]{0,2,1:T(8,128)(2,1)S(1)} %get-tuple-element.202), kind=kLoop, calls=%fused_computation.8.clone.1 | loop fusion | flops 4915200 | bytes 13110400 | tf_op jit(solution)/shard_map/convert.1
  163.9 3.9 %bitcast_dynamic-update-slice_fusion.2 = (bf16[5,4,2560]{2,1,0:T(4,128)(2,1)S(1)}, bf16[4,2560]{1,0:T(4,128)(2,1)}) fusion(bf16[5,4,2560]{2,1,0:T(4,128)(2,1)S(1)} %get-tuple-element.220, s32[]{:T(128)} %get-tuple-element.219, bf16[640,2560]{0,1:T(8,128)(2,1)} %get-tuple-element.203, bf16[640,2560]{0,1:T(8,128)(2,1)S(1)} %get-tuple-element.204, ...), kind=kOutput, calls=%fused_computation.43.clone.1 | convolution fusion | flops 39352320 | bytes 6608900 | tf_op jit(solution)/shard_map/while/body/eval_jaxpr/dot_general | solution.py:78
  175.8 11.7 %all-to-all-start.2 = ((bf16[64,2,200]{2,1,0:T(2,128)(2,1)}), bf16[64,2,200]{2,1,0:T(2,128)(2,1)S(1)}, u32[]{:S(2)}, u32[]{:S(2)}) async-start(bf16[64,2,200]{2,1,0:T(2,128)(2,1)} %reshape.464), calls=%async_computation.2 | async-start | bytes 131072 | tf_op jit(solution)/shard_map/all_to_all | solution.py:93
  187.6 10.1 %all-to-all-done.2 = bf16[64,2,200]{2,1,0:T(2,128)(2,1)S(1)} async-done(((bf16[64,2,200]{2,1,0:T(2,128)(2,1)}), bf16[64,2,200]{2,1,0:T(2,128)(2,1)S(1)}, u32[]{:S(2)}, u32[]{:S(2)}) %all-to-all-start.2) | async-done | bytes 51232 | tf_op jit(solution)/shard_map/all_to_all | solution.py:93
  198.5 5.7 %copy.89 = bf16[5,4,2,64,10]{4,3,2,1,0:T(8,128)(2,1)S(1)} copy(bf16[5,4,2,64,10]{0,1,2,4,3:T(4,128)(2,1)S(1)} %bitcast.113) | data formatting | bytes 102400 | tf_op jit(solution)/shard_map/all_to_all | solution.py:93
  206.2 3.3 %all-to-all-start.3 = ((bf16[320,4,2,10]{0,2,3,1:T(2,128)(2,1)}), bf16[320,4,2,10]{0,2,3,1:T(2,128)(2,1)S(1)}, u32[]{:S(2)}, u32[]{:S(2)}) async-start(bf16[320,4,2,10]{0,2,3,1:T(2,128)(2,1)} %copy.81), calls=%async_computation.3 | async-start | bytes 122880 | tf_op jit(solution)/shard_map/all_to_all | solution.py:92
  209.5 4.4 %all-to-all-done.3 = bf16[320,4,2,10]{0,2,3,1:T(2,128)(2,1)S(1)} async-done(((bf16[320,4,2,10]{0,2,3,1:T(2,128)(2,1)}), bf16[320,4,2,10]{0,2,3,1:T(2,128)(2,1)S(1)}, u32[]{:S(2)}, u32[]{:S(2)}) %all-to-all-start.3) | async-done | bytes 51232 | tf_op jit(solution)/shard_map/all_to_all | solution.py:92
  214.4 4.4 %gather_fusion.4 = bf16[1280,2,10]{2,1,0:T(2,128)(2,1)S(1)} fusion(bf16[1280,2,10]{2,1,0:T(2,128)(2,1)S(1)} %bitcast.114, s32[2048]{0:T(1024)S(1)} %pad_clamp_fusion), kind=kCustom, calls=%fused_computation.4 | custom fusion | bytes 107520 | tf_op jit(solution)/shard_map/jit(_take)/gather | solution.py:104
  219.4 5.6 %fusion.42 = f32[5,2,2,1,641]{4,2,0,3,1:T(2,128)S(1)} fusion(bf16[5,641,1280]{2,1,0:T(8,128)(2,1)} %param.10, bf16[1280,2,5,2]{0,1,3,2:T(2,128)(2,1)S(1)} %bitcast.119, pred[1280]{0:T(1024)(128)(4,1)S(1)} %compare_and_fusion), kind=kOutput, calls=%fused_computation.62 | convolution fusion | flops 32844800 | bytes 8308560 | tf_op jit(solution)/shard_map/qlrps,pcq->psrlc/dot_general | solution.py:35
  (129 shorter events, 63.8 us)
Async XLA Ops:
  0.6 47.9 %copy-start = (f32[1280]{0:T(1024)S(1)}, f32[1280]{0:T(1024)}, u32[]{:S(2)}) copy-start(f32[1280]{0:T(1024)} %param.12) | copy-start | bytes 15364
  3.8 31.9 %copy-start.3 = (s32[640]{0:T(1024)S(1)}, s32[640]{0:T(1024)}, u32[]{:S(2)}) copy-start(s32[640]{0:T(1024)} %param.13) | copy-start | bytes 7684
  3.8 32.0 %copy-start.1 = (s32[1280]{0:T(1024)S(1)}, s32[1280]{0:T(1024)}, u32[]{:S(2)}) copy-start(s32[1280]{0:T(1024)} %param.14) | copy-start | bytes 15364
  19.1 30.1 %copy-start.2 = (s32[1280]{0:T(1024)S(1)}, s32[1280]{0:T(1024)}, u32[]{:S(2)}) copy-start(s32[1280]{0:T(1024)} %param.15) | copy-start | bytes 15364
  22.5 27.4 %all-to-all-start = ((bf16[64,2,200]{2,1,0:T(2,128)(2,1)}), bf16[64,2,200]{2,1,0:T(2,128)(2,1)S(1)}, u32[]{:S(2)}, u32[]{:S(2)}) async-start(bf16[64,2,200]{2,1,0:T(2,128)(2,1)} %reshape.462), calls=%async_computation | async-start | bytes 131072 | tf_op jit(solution)/shard_map/all_to_all | solution.py:64
  58.0 8.4 %all-to-all-start.1 = ((bf16[4,5,1,2,640]{4,3,1,2,0:T(2,128)(2,1)}), bf16[4,5,1,2,640]{4,3,1,2,0:T(2,128)(2,1)S(1)}, u32[]{:S(2)}, u32[]{:S(2)}) async-start(bf16[4,5,1,2,640]{4,3,1,2,0:T(2,128)(2,1)} %pad_maximum_fusion.9), calls=%async_computation.1 | async-start | bytes 102400 | tf_op jit(solution)/shard_map/all_to_all | solution.py:66
  172.0 53.0 %copy-start.4 = (bf16[5,4,2560]{2,1,0:T(4,128)(2,1)}, bf16[5,4,2560]{2,1,0:T(4,128)(2,1)S(1)}, u32[]{:S(2)}) copy-start(bf16[5,4,2560]{2,1,0:T(4,128)(2,1)S(1)} %get-tuple-element.96) | copy-start | bytes 307204
  175.8 21.8 %all-to-all-start.2 = ((bf16[64,2,200]{2,1,0:T(2,128)(2,1)}), bf16[64,2,200]{2,1,0:T(2,128)(2,1)S(1)}, u32[]{:S(2)}, u32[]{:S(2)}) async-start(bf16[64,2,200]{2,1,0:T(2,128)(2,1)} %reshape.464), calls=%async_computation.2 | async-start | bytes 131072 | tf_op jit(solution)/shard_map/all_to_all | solution.py:93
  206.2 7.7 %all-to-all-start.3 = ((bf16[320,4,2,10]{0,2,3,1:T(2,128)(2,1)}), bf16[320,4,2,10]{0,2,3,1:T(2,128)(2,1)S(1)}, u32[]{:S(2)}, u32[]{:S(2)}) async-start(bf16[320,4,2,10]{0,2,3,1:T(2,128)(2,1)} %copy.81), calls=%async_computation.3 | async-start | bytes 122880 | tf_op jit(solution)/shard_map/all_to_all | solution.py:92
